TPU v7x, 512 devices: a whole 4x8x8 slice. The times are simulated.
512 devices in a mesh: blk: 64 (over x, y_hi, z), head: 8 (over y_lo, core).
Axes of the slice: x: 4, y: 8 (y_hi: 2, y_lo: 4; y = y_hi * 4 + y_lo), z: 8, core: 2. Of those that a mesh axis runs over, the one named last changes fastest.
Arguments:
- query_rows: bfloat16 [16384, 2048], P('blk', 'head'), may hold values from -10 to 10
- key_rows: bfloat16 [16384, 2048], P('blk', 'head'), may hold values from -10 to 10
- value_rows: bfloat16 [16384, 2048], P('blk', 'head'), may hold values from -6 to 6
- grad_out: bfloat16 [16384, 4096], P('blk', 'head'), may hold values from -6 to 6
- out_weight: bfloat16 [2048, 4096], P('head'), may hold values from -0.09375 to 0.09375
- mask_types: int32 [128, 128], replicated, may hold values from 0 to 2, as said below
- drop_seed: int32 [1], replicated, may hold values from 0 to 1048575
Outputs:
- grad_query: bfloat16 [16384, 2048], P('blk', 'head')
- grad_key: bfloat16 [16384, 2048], P('blk', 'head')
- grad_value: bfloat16 [16384, 2048], P('blk', 'head')
Inputs may be any that keep to these rules, and one draw needn't show every extreme that they name: Blocks are runs of 128 positions. The sequence is cut into documents of whole blocks, each 1 to 4 blocks long, and some document has exactly 4 blocks. Images are pairs of blocks 2m and 2m + 1 of one document. mask_types[a, b] is 0 where blocks a and b lie in different documents; inside a document it is 2 for b < a, 2 for b = a in an image, 1 for b = a in text, 2 for b = a + 1 in one image, and 0 for other b > a. So a position sees keys only of its own shard of 256 positions and of up to 2 earlier ones.
All inputs are finite; a program needn't handle non-finite values.
Results may differ from a plain program's by a relative error of at most 0.029.
Values may be sent and summed in bfloat16 or wider, within the bound.
No kernel may reach another device: no remote copies, remote signals or barrier semaphores. Data moves between devices by JAX's collectives and lax.ppermute only.
A program may use at most 64 MiB of HBM per device.

v0:
```python
import jax
import jax.numpy as jnp
from jax import lax
from jax.sharding import PartitionSpec as P

DH = 128
HEADS_DEV = 2
MB = 128
REACH = 2
drop_level = 6554
keep_scale = 65536.0 / 58982.0
mix_one = 73244475
mix_two = 295559667
mix_three = 668265263


def shifted(value, axis, steps):
    count = lax.axis_size(axis)
    leading, last = (max(0, -steps), min(count, count - steps))
    return lax.ppermute(value, axis, [(source, source + steps) for source in range(leading, last)])


def mixhash(seed_word, head_index, query_pos, key_pos):
    hashed = query_pos * mix_one + key_pos * mix_two + head_index * mix_three + seed_word
    hashed = hashed ^ lax.shift_right_logical(hashed, jnp.int32(16))
    hashed = hashed * mix_one
    hashed = hashed ^ lax.shift_right_logical(hashed, jnp.int32(16))
    hashed = hashed * mix_one
    hashed = hashed ^ lax.shift_right_logical(hashed, jnp.int32(16))
    return (hashed & 65535 >= drop_level).astype(jnp.float32)


def visible(table_tile, query_pos, key_pos):
    return (table_tile == 2) | (table_tile == 1) & (key_pos[None, :] <= query_pos[:, None])


def expand(block_table):
    count_rows, count_cols = block_table.shape
    spread = jnp.broadcast_to(block_table[:, None, :, None], (count_rows, MB, count_cols, MB))
    return spread.reshape(count_rows * MB, count_cols * MB)


def contract_first(left, right):
    return lax.dot_general(
        left, right, (((0,), (0,)), ((), ())), preferred_element_type=jnp.float32
    )


def contract_last(left, right):
    return lax.dot_general(
        left, right, (((1,), (1,)), ((), ())), preferred_element_type=jnp.float32
    )


def on_device(query_rows, key_rows, value_rows, grad_out, out_weight, mask_types, drop_seed):
    row_count = query_rows.shape[0]
    span_rows = (REACH + 1) * row_count
    block_rows = row_count // MB
    margin_blocks = REACH * block_rows
    span_blocks = span_rows // MB
    score_scale = DH ** (-0.5)
    seed_word = drop_seed[0]
    device = lax.axis_index("blk")
    head_base = lax.axis_index("head") * HEADS_DEV
    own_pos = device * row_count + jnp.arange(row_count, dtype=jnp.int32)
    window_pos = (device - REACH) * row_count + jnp.arange(span_rows, dtype=jnp.int32)
    padded_table = jnp.pad(mask_types, margin_blocks)
    near_table = lax.dynamic_slice(
        padded_table,
        (device * block_rows + margin_blocks, device * block_rows),
        (block_rows, span_blocks),
    )
    allowed = visible(expand(near_table), own_pos, window_pos)
    grad_attn = contract_last(
        lax.all_gather(grad_out, "head", axis=1, tiled=True), out_weight
    ).astype(jnp.bfloat16)
    offsets = [distance for distance in range(1, REACH + 1)]
    stacked = jnp.stack((key_rows, value_rows))
    key_slots = [stacked for slot_index in range(REACH + 1)]
    for distance in offsets:
        key_slots[REACH - distance] = shifted(stacked, "blk", distance)
    windowed = jnp.concatenate(key_slots, axis=1)
    query_grads = []
    key_parts = []
    value_parts = []
    total_cols = []
    dot_cols = []
    for local_head in range(HEADS_DEV):
        head_index = head_base + local_head
        first_col = local_head * DH
        last_col = first_col + DH
        query_head = query_rows[:, first_col:last_col]
        grad_head = grad_attn[:, first_col:last_col]
        key_window = windowed[0, :, first_col:last_col]
        value_window = windowed[1, :, first_col:last_col]
        scores = contract_last(query_head, key_window) * score_scale
        masked = jnp.where(allowed, scores, -jnp.inf)
        row_max = jnp.max(masked, axis=1, keepdims=True)
        log_total = row_max + jnp.log(jnp.sum(jnp.exp(masked - row_max), axis=1, keepdims=True))
        attn_prob = jnp.where(allowed, jnp.exp(scores - log_total), 0.0)
        keep_mask = (
            mixhash(seed_word, head_index, own_pos[:, None], window_pos[None, :]) * keep_scale
        )
        dropped = (attn_prob * keep_mask).astype(jnp.bfloat16)
        attended = jnp.dot(dropped, value_window, preferred_element_type=jnp.float32).astype(
            jnp.bfloat16
        )
        row_dot = jnp.sum(
            grad_head.astype(jnp.float32) * attended.astype(jnp.float32), axis=1, keepdims=True
        )
        grad_prob = contract_last(grad_head, value_window)
        dscore = (attn_prob * (grad_prob * keep_mask - row_dot)).astype(jnp.bfloat16)
        query_grads.append(
            jnp.dot(dscore, key_window, preferred_element_type=jnp.float32) * score_scale
        )
        total_cols.append(log_total)
        dot_cols.append(row_dot)
        key_parts.append(contract_first(dscore, query_head) * score_scale)
        value_parts.append(contract_first(dropped, grad_head))
    grad_query = jnp.concatenate(query_grads, axis=1).astype(jnp.bfloat16)
    partials = jnp.stack((jnp.concatenate(key_parts, axis=1), jnp.concatenate(value_parts, axis=1)))
    summed = partials[:, REACH * row_count : (REACH + 1) * row_count]
    for distance in offsets:
        slot_index = REACH - distance
        outgoing = partials[:, slot_index * row_count : (slot_index + 1) * row_count]
        summed = summed + shifted(outgoing, "blk", -distance)
    grad_key = summed[0].astype(jnp.bfloat16)
    grad_value = summed[1].astype(jnp.bfloat16)
    return (grad_query, grad_key, grad_value)


def solution(mesh):
    in_specs = (
        P("blk", "head"),
        P("blk", "head"),
        P("blk", "head"),
        P("blk", "head"),
        P("head", None),
        P(),
        P(),
    )
    out_specs = (P("blk", "head"), P("blk", "head"), P("blk", "head"))
    return jax.shard_map(
        on_device, mesh=mesh, in_specs=in_specs, out_specs=out_specs, check_vma=False
    )
```

profile of v0, /device:TPU:6, one launch (start us, length us, event | category | flops | bytes accessed | tf_op | source)
XLA Modules:
  0.0 147.7 jit_solution(5357728235868405602)
XLA Ops:
  7.2 0.0 copy-start
  7.2 0.0 copy-start.6
  7.2 0.0 copy-start.7
  7.2 0.0 all-gather.2.cloned.1.call-start
  7.2 0.7 all-gather.2.cloned.1.call-update
  7.9 1.0 pad_maximum_fusion.1
  8.9 4.3 %collective-permute-start.1 = (bf16[2,256,256]{2,1,0:T(8,128)(2,1)S(1)}, bf16[2,256,256]{2,1,0:T(8,128)(2,1)S(1)}, u32[]{:S(2)}, u32[]{:S(2)}) collective-permute-start(bf16[2,256,256]{2,1,0:T(8,128)(2,1)S(1)} %pad_maximum_fusion.1), channel_id=1, source_target_pairs={{0,8},{8,16},{16,24},{24,32},{32,40},{40,48},{48,56},{56,64},{64,7... | collective-permute-start | bytes 786440 | tf_op jit(solution)/shard_map/ppermute | solution.py:20
  13.2 6.1 %collective-permute-start = (bf16[2,256,256]{2,1,0:T(8,128)(2,1)S(1)}, bf16[2,256,256]{2,1,0:T(8,128)(2,1)S(1)}, u32[]{:S(2)}, u32[]{:S(2)}) collective-permute-start(bf16[2,256,256]{2,1,0:T(8,128)(2,1)S(1)} %pad_maximum_fusion.1), channel_id=1, source_target_pairs={{0,16},{8,24},{16,32},{24,40},{32,48},{40,56},{48,64},{56,72},{64,... | collective-permute-start | bytes 786440 | tf_op jit(solution)/shard_map/ppermute | solution.py:20
  19.3 0.8 broadcast_compare_fusion
  20.8 0.1 broadcast_in_dim.13
  20.9 0.1 copy.31
  21.1 0.0 copy-start.8
  21.1 0.3 copy.18
  21.4 0.1 broadcast_in_dim.14
  21.5 0.1 copy.30
  21.6 1.0 copy.17
  22.6 0.0 copy-start.9
  22.6 13.1 %collective-permute-done.1 = bf16[2,256,256]{2,1,0:T(8,128)(2,1)S(1)} collective-permute-done((bf16[2,256,256]{2,1,0:T(8,128)(2,1)S(1)}, bf16[2,256,256]{2,1,0:T(8,128)(2,1)S(1)}, u32[]{:S(2)}, u32[]{:S(2)}) %collective-permute-start.1) | collective-permute-done | bytes 262176 | tf_op jit(solution)/shard_map/ppermute | solution.py:20
  35.7 5.8 %collective-permute-done = bf16[2,256,256]{2,1,0:T(8,128)(2,1)S(1)} collective-permute-done((bf16[2,256,256]{2,1,0:T(8,128)(2,1)S(1)}, bf16[2,256,256]{2,1,0:T(8,128)(2,1)S(1)}, u32[]{:S(2)}, u32[]{:S(2)}) %collective-permute-start) | collective-permute-done | bytes 262176 | tf_op jit(solution)/shard_map/ppermute | solution.py:20
  41.5 0.0 copy-done.6
  41.5 0.0 copy-done.7
  41.5 0.1 maximum_maximum_fusion
  41.6 0.0 copy-done.8
  41.6 0.0 copy-start.2
  41.6 0.3 fusion.4
  41.9 0.0 copy-done.9
  41.9 0.5 fusion.33
  42.4 0.1 copy-done.2
  42.5 0.0 copy-start.4
  42.5 0.9 copy-done.4
  43.4 0.3 exponential_reduce_fusion.1
  43.7 12.8 %all-gather.2.cloned.1.call-done = bf16[256,4096]{1,0:T(8,128)(2,1)} async-done(((bf16[256,512]{1,0:T(8,128)(2,1)}), bf16[256,4096]{1,0:T(8,128)(2,1)}) %all-gather.2.cloned.1.call-update) | async-done | bytes 2097168 | tf_op jit(solution)/shard_map/all_gather | solution.py:75
  56.6 0.0 copy-done
  56.6 0.0 copy-start.3
  56.6 0.0 copy-start.5
  56.6 2.4 %convolution_convert_fusion = bf16[256,256]{0,1:T(8,128)(2,1)S(1)} fusion(bf16[256,4096]{1,0:T(8,128)(2,1)} %all-gather.2.cloned.1.call-done, bf16[256,4096]{1,0:T(8,128)(2,1)S(1)} %copy-done), kind=kOutput, calls=%fused_computation.24 | convolution fusion | flops 536936448 | bytes 4325376 | tf_op jit(solution)/shard_map/dot_general | solution.py:50
  59.0 0.0 copy-done.3
  59.0 0.0 copy-done.5
  59.0 0.8 fusion.15
  59.9 0.8 fusion.42
  60.6 0.7 fusion.6
  61.4 0.3 convolution_multiply_fusion.5
  61.6 0.8 fusion.14
  62.5 0.8 fusion.39
  63.2 0.7 fusion.7
  64.0 0.3 convolution_multiply_fusion.4
  64.2 0.1 maximum_bitcast_fusion.1
  64.3 0.1 maximum_bitcast_fusion
  64.4 0.0 copy-start.1
  64.4 1.0 fusion.28
  65.4 18.8 %collective-permute-start.2 = (f32[2,256,256]{1,2,0:T(8,128)}, f32[2,256,256]{1,2,0:T(8,128)}, u32[]{:S(2)}, u32[]{:S(2)}) collective-permute-start(f32[2,256,256]{1,2,0:T(8,128)} %get-tuple-element.16), channel_id=1, source_target_pairs={{8,0},{16,8},{24,16},{32,24},{40,32},{48,40},{56,48},{64,56},{72,6... | collective-permute-start | bytes 1572872 | tf_op jit(solution)/shard_map/ppermute | solution.py:20
  84.2 1.9 %collective-permute-start.3 = (f32[2,256,256]{1,2,0:T(8,128)S(1)}, f32[2,256,256]{1,2,0:T(8,128)}, u32[]{:S(2)}, u32[]{:S(2)}) collective-permute-start(f32[2,256,256]{1,2,0:T(8,128)S(1)} %get-tuple-element.17), channel_id=1, source_target_pairs={{16,0},{24,8},{32,16},{40,24},{48,32},{56,40},{64,48},{72,56},{80,... | collective-permute-start | bytes 1572872 | tf_op jit(solution)/shard_map/ppermute | solution.py:20
  86.2 0.3 fusion.8
  86.4 0.0 copy-done.1
  86.5 0.3 fusion.9
  86.7 0.8 copy.21
  87.5 40.2 %collective-permute-done.2 = f32[2,256,256]{1,2,0:T(8,128)} collective-permute-done((f32[2,256,256]{1,2,0:T(8,128)}, f32[2,256,256]{1,2,0:T(8,128)}, u32[]{:S(2)}, u32[]{:S(2)}) %collective-permute-start.2) | collective-permute-done | bytes 524320 | tf_op jit(solution)/shard_map/ppermute | solution.py:20
  127.7 10.3 %collective-permute-done.3 = f32[2,256,256]{1,2,0:T(8,128)} collective-permute-done((f32[2,256,256]{1,2,0:T(8,128)S(1)}, f32[2,256,256]{1,2,0:T(8,128)}, u32[]{:S(2)}, u32[]{:S(2)}) %collective-permute-start.3) | collective-permute-done | bytes 524320 | tf_op jit(solution)/shard_map/ppermute | solution.py:20
  138.0 1.3 fusion.32
  139.3 0.8 copy.23
  140.1 0.8 copy.22
  (8 shorter events, 0.1 us)
Async XLA Ops:
  7.2 49.4 %copy-start = (bf16[256,4096]{1,0:T(8,128)(2,1)S(1)}, bf16[256,4096]{1,0:T(8,128)(2,1)}, u32[]{:S(2)}) copy-start(bf16[256,4096]{1,0:T(8,128)(2,1)} %param.11) | copy-start | bytes 6291460
  7.2 34.4 %copy-start.6 = (bf16[256,256]{1,0:T(8,128)(2,1)S(1)}, bf16[256,256]{1,0:T(8,128)(2,1)}, u32[]{:S(2)}) copy-start(bf16[256,256]{1,0:T(8,128)(2,1)} %param.9) | copy-start | bytes 393220
  7.2 34.4 %copy-start.7 = (bf16[256,256]{1,0:T(8,128)(2,1)S(1)}, bf16[256,256]{1,0:T(8,128)(2,1)}, u32[]{:S(2)}) copy-start(bf16[256,256]{1,0:T(8,128)(2,1)} %param.8) | copy-start | bytes 393220
  7.2 49.4 %all-gather.2.cloned.1.call-start = ((), (), s32[]{:S(2)}) async-start(), calls=%async_computation | async-start | bytes 2359296 | tf_op jit(solution)/shard_map/all_gather | solution.py:75
  8.9 26.8 %collective-permute-start.1 = (bf16[2,256,256]{2,1,0:T(8,128)(2,1)S(1)}, bf16[2,256,256]{2,1,0:T(8,128)(2,1)S(1)}, u32[]{:S(2)}, u32[]{:S(2)}) collective-permute-start(bf16[2,256,256]{2,1,0:T(8,128)(2,1)S(1)} %pad_maximum_fusion.1), channel_id=1, source_target_pairs={{0,8},{8,16},{16,24},{24,32},{32,40},{40,48},{48,56},{56,64},{64,7... | collective-permute-start | bytes 786440 | tf_op jit(solution)/shard_map/ppermute | solution.py:20
  13.2 28.3 %collective-permute-start = (bf16[2,256,256]{2,1,0:T(8,128)(2,1)S(1)}, bf16[2,256,256]{2,1,0:T(8,128)(2,1)S(1)}, u32[]{:S(2)}, u32[]{:S(2)}) collective-permute-start(bf16[2,256,256]{2,1,0:T(8,128)(2,1)S(1)} %pad_maximum_fusion.1), channel_id=1, source_target_pairs={{0,16},{8,24},{16,32},{24,40},{32,48},{40,56},{48,64},{56,72},{64,... | collective-permute-start | bytes 786440 | tf_op jit(solution)/shard_map/ppermute | solution.py:20
  21.1 20.6 %copy-start.8 = (bf16[256,256]{1,0:T(8,128)(2,1)S(1)}, bf16[256,256]{1,0:T(8,128)(2,1)}, u32[]{:S(2)}) copy-start(bf16[256,256]{1,0:T(8,128)(2,1)} %param.7) | copy-start | bytes 393220
  22.6 19.3 %copy-start.9 = (pred[256,768]{0,1:T(32,128)(4,1)S(1)}, pred[256,768]{0,1:T(32,128)(4,1)}, u32[]{:S(2)}) copy-start(pred[256,768]{0,1:T(32,128)(4,1)} %copy.17) | copy-start | bytes 589828
  41.6 0.9 copy-start.2
  42.5 0.9 copy-start.4
  56.6 2.5 %copy-start.3 = (bf16[2,768,256]{2,1,0:T(8,128)(2,1)S(1)}, bf16[2,768,256]{2,1,0:T(8,128)(2,1)}, u32[]{:S(2)}) copy-start(bf16[2,768,256]{2,1,0:T(8,128)(2,1)} %copy-done.2) | copy-start | bytes 2359300
  56.6 2.5 %copy-start.5 = (f32[256,768]{0,1:T(8,128)S(1)}, f32[256,768]{0,1:T(8,128)}, u32[]{:S(2)}) copy-start(f32[256,768]{0,1:T(8,128)} %copy-done.4) | copy-start | bytes 2359300
  64.4 22.1 %copy-start.1 = (f32[1,768,256]{1,2,0:T(8,128)}, f32[1,768,256]{1,2,0:T(8,128)S(1)}, u32[]{:S(2)}) copy-start(f32[1,768,256]{1,2,0:T(8,128)S(1)} %maximum_bitcast_fusion) | copy-start | bytes 2359300
  65.4 62.3 %collective-permute-start.2 = (f32[2,256,256]{1,2,0:T(8,128)}, f32[2,256,256]{1,2,0:T(8,128)}, u32[]{:S(2)}, u32[]{:S(2)}) collective-permute-start(f32[2,256,256]{1,2,0:T(8,128)} %get-tuple-element.16), channel_id=1, source_target_pairs={{8,0},{16,8},{24,16},{32,24},{40,32},{48,40},{56,48},{64,56},{72,6... | collective-permute-start | bytes 1572872 | tf_op jit(solution)/shard_map/ppermute | solution.py:20
  84.2 53.7 %collective-permute-start.3 = (f32[2,256,256]{1,2,0:T(8,128)S(1)}, f32[2,256,256]{1,2,0:T(8,128)}, u32[]{:S(2)}, u32[]{:S(2)}) collective-permute-start(f32[2,256,256]{1,2,0:T(8,128)S(1)} %get-tuple-element.17), channel_id=1, source_target_pairs={{16,0},{24,8},{32,16},{40,24},{48,32},{56,40},{64,48},{72,56},{80,... | collective-permute-start | bytes 1572872 | tf_op jit(solution)/shard_map/ppermute | solution.py:20
Sparse Core Ops, SparseCore 0:
  10.1 46.3 all-gather.1
where the time goes:
time: 148 us
  waiting for transfers between devices  82.9 us (56%)
  starting transfers between devices  31.2 us (21%)
  between operations  15 us (10%)
  matrix products  8.92 us (6%)
  local copies, waits for them, and re-layouts  5.06 us (3%)
  other arithmetic  4.67 us (3%)
    ppermute x4, waiting for transfers between devices, shifted(): lax.ppermute(value, axis, [(source, source + steps) for source in range(l...  69.4 us
    ppermute x4, starting transfers between devices, shifted(): lax.ppermute(value, axis, [(source, source + steps) for source in range(l...  31.1 us
    all_gather x1, waiting for transfers between devices, on_device(): lax.all_gather(grad_out, 'head', axis=1, tiled=True)  12.8 us
    dot_general x5, matrix products, contract_last(): lax.dot_general(left, right, (((1,), (1,)), ((), ())), preferred_element_...  4.61 us
    unnamed x25, local copies, waits for them, and re-layouts  3.5 us
  transfers between devices with their start and end apart: 5, of which 5 were waited for; matrix products, arithmetic and copies ran while one was open for 4% of the time, Pallas kernels for 0%

commit v1 on v0

--- a/solution.py
+++ b/solution.py
@@ -2,6 +2,7 @@
 import jax.numpy as jnp
 from jax import lax
 from jax.sharding import PartitionSpec as P
+from jax.lax import all_to_all, psum
 
 DH = 128
 HEADS_DEV = 2
@@ -71,9 +72,10 @@
         (block_rows, span_blocks),
     )
     allowed = visible(expand(near_table), own_pos, window_pos)
-    grad_attn = contract_last(
-        lax.all_gather(grad_out, "head", axis=1, tiled=True), out_weight
-    ).astype(jnp.bfloat16)
+    packet_extend = lambda block_here: jnp.concatenate(
+        all_to_all(jnp.stack(psum(1, "head") * [block_here]), "head", 0, 0), 1
+    )
+    grad_attn = contract_last(packet_extend(grad_out), out_weight).astype(jnp.bfloat16)
     offsets = [distance for distance in range(1, REACH + 1)]
     stacked = jnp.stack((key_rows, value_rows))
     key_slots = [stacked for slot_index in range(REACH + 1)]

time: 148 us -> 153 us (1.034)
  the two profiles are of different devices: /device:TPU:6 before, /device:TPU:2 now
where the time goes in v1:
time: 153 us; the launch traced here: 152 us
  waiting for transfers between devices  95.1 us (62%)
  starting transfers between devices  35.7 us (23%)
  matrix products  8.81 us (6%)
  local copies, waits for them, and re-layouts  7.87 us (5%)
  other arithmetic  3.01 us (2%)
  between operations  1.63 us (1%)
    ppermute x4, waiting for transfers between devices, shifted(): lax.ppermute(value, axis, [(source, source + steps) for source in range(l...  95.1 us
    ppermute x4, starting transfers between devices, shifted(): lax.ppermute(value, axis, [(source, source + steps) for source in range(l...  30.7 us
    all_to_all x1, starting transfers between devices, on_device(): all_to_all(jnp.stack(psum(1, 'head') * [block_here]), 'head', 0, 0)  5.01 us
    unnamed x28, local copies, waits for them, and re-layouts  4.9 us
    dot_general x5, matrix products, contract_last(): lax.dot_general(left, right, (((1,), (1,)), ((), ())), preferred_element_...  4.5 us
  transfers between devices with their start and end apart: 5, of which 3 were waited for; matrix products, arithmetic and copies ran while one was open for 3% of the time, Pallas kernels for 0%

profile of v1, /device:TPU:2, one launch (start us, length us, event | category | flops | bytes accessed | tf_op | source)
XLA Modules:
  0.0 152.1 jit_solution(4348371017736450569)
XLA Ops:
  0.6 0.0 copy-start
  0.6 1.2 copy.19
  1.9 1.4 stack.32
  3.3 0.0 copy-start.6
  3.3 0.0 copy-start.7
  3.3 0.0 copy-start.10
  3.3 5.0 %all-to-all-start = ((bf16[8,256,512]{1,2,0:T(8,128)(2,1)}), bf16[8,256,512]{1,2,0:T(8,128)(2,1)}, u32[]{:S(2)}, u32[]{:S(2)}) async-start(bf16[8,256,512]{1,2,0:T(8,128)(2,1)} %stack.32), calls=%async_computation | async-start | bytes 4194304 | tf_op jit(solution)/shard_map/all_to_all | solution.py:76
  8.3 0.0 copy-done.6
  8.3 0.0 copy-done.7
  8.4 4.3 %collective-permute-start.1 = (bf16[2,256,256]{2,1,0:T(8,128)(2,1)S(1)}, bf16[2,256,256]{2,1,0:T(8,128)(2,1)S(1)}, u32[]{:S(2)}, u32[]{:S(2)}) collective-permute-start(bf16[2,256,256]{2,1,0:T(8,128)(2,1)S(1)} %pad_maximum_fusion.1), channel_id=1, source_target_pairs={{0,8},{8,16},{16,24},{24,32},{32,40},{40,48},{48,56},{56,64},{64,7... | collective-permute-start | bytes 786440 | tf_op jit(solution)/shard_map/ppermute | solution.py:21
  12.7 6.1 %collective-permute-start = (bf16[2,256,256]{2,1,0:T(8,128)(2,1)S(1)}, bf16[2,256,256]{2,1,0:T(8,128)(2,1)S(1)}, u32[]{:S(2)}, u32[]{:S(2)}) collective-permute-start(bf16[2,256,256]{2,1,0:T(8,128)(2,1)S(1)} %pad_maximum_fusion.1), channel_id=1, source_target_pairs={{0,16},{8,24},{16,32},{24,40},{32,48},{40,56},{48,64},{56,72},{64,... | collective-permute-start | bytes 786440 | tf_op jit(solution)/shard_map/ppermute | solution.py:21
  18.8 0.0 copy-done.10
  18.8 0.1 broadcast_compare_fusion
  18.9 0.1 broadcast_in_dim.13
  19.0 0.1 copy.32
  19.2 0.0 copy-start.8
  19.2 0.3 copy.18
  19.5 0.1 broadcast_in_dim.14
  19.6 0.1 copy.31
  19.7 1.0 copy.17
  21.3 0.0 copy-start.9
  21.4 53.5 %collective-permute-done.1 = bf16[2,256,256]{2,1,0:T(8,128)(2,1)S(1)} collective-permute-done((bf16[2,256,256]{2,1,0:T(8,128)(2,1)S(1)}, bf16[2,256,256]{2,1,0:T(8,128)(2,1)S(1)}, u32[]{:S(2)}, u32[]{:S(2)}) %collective-permute-start.1) | collective-permute-done | bytes 262176 | tf_op jit(solution)/shard_map/ppermute | solution.py:21
  74.9 0.0 collective-permute-done
  74.9 0.1 maximum_maximum_fusion
  74.9 0.0 copy-done.8
  74.9 0.0 copy-start.2
  75.0 0.3 fusion.4
  75.2 0.0 copy-done.9
  75.2 0.5 fusion.33
  75.7 0.1 copy-done.2
  75.8 0.0 copy-start.4
  75.8 0.9 copy-done.4
  76.7 0.3 exponential_reduce_fusion.1
  77.1 0.0 all-to-all-done
  77.1 0.0 copy-done
  77.1 0.0 copy-start.3
  77.1 2.4 %convolution_convert_fusion = bf16[256,256]{0,1:T(8,128)(2,1)S(1)} fusion(bf16[256,4096]{1,0:T(8,128)(2,1)S(1)} %copy-done, bf16[256,4096]{0,1:T(8,128)(2,1)} %bitcast.5), kind=kOutput, calls=%fused_computation.24 | convolution fusion | flops 536936448 | bytes 4325376 | tf_op jit(solution)/shard_map/dot_general | solution.py:51
  79.5 0.0 copy-done.3
  79.5 0.8 fusion.14
  80.3 0.0 copy-start.5
  80.3 0.7 fusion.7
  81.0 0.3 convolution_multiply_fusion.4
  81.3 0.1 copy-done.5
  81.5 0.8 fusion.15
  82.3 0.7 fusion.6
  83.0 0.3 convolution_multiply_fusion.5
  83.3 0.8 fusion.39
  84.0 0.8 fusion.42
  84.8 0.1 maximum_bitcast_fusion
  84.9 0.1 maximum_bitcast_fusion.1
  84.9 0.0 copy-start.1
  85.0 1.0 fusion.28
  86.0 7.2 %collective-permute-start.3 = (f32[2,256,256]{1,2,0:T(8,128)}, f32[2,256,256]{1,2,0:T(8,128)}, u32[]{:S(2)}, u32[]{:S(2)}) collective-permute-start(f32[2,256,256]{1,2,0:T(8,128)} %get-tuple-element.17), channel_id=1, source_target_pairs={{16,0},{24,8},{32,16},{40,24},{48,32},{56,40},{64,48},{72,56},{80,... | collective-permute-start | bytes 1572872 | tf_op jit(solution)/shard_map/ppermute | solution.py:21
  93.2 13.2 %collective-permute-start.2 = (f32[2,256,256]{1,2,0:T(8,128)S(1)}, f32[2,256,256]{1,2,0:T(8,128)}, u32[]{:S(2)}, u32[]{:S(2)}) collective-permute-start(f32[2,256,256]{1,2,0:T(8,128)S(1)} %get-tuple-element.16), channel_id=1, source_target_pairs={{8,0},{16,8},{24,16},{32,24},{40,32},{48,40},{56,48},{64,56},{72,6... | collective-permute-start | bytes 1572872 | tf_op jit(solution)/shard_map/ppermute | solution.py:21
  106.3 0.3 fusion.9
  106.6 0.0 copy-done.1
  106.6 0.3 fusion.8
  106.9 0.8 copy.22
  107.7 28.6 %collective-permute-done.3 = f32[2,256,256]{1,2,0:T(8,128)} collective-permute-done((f32[2,256,256]{1,2,0:T(8,128)}, f32[2,256,256]{1,2,0:T(8,128)}, u32[]{:S(2)}, u32[]{:S(2)}) %collective-permute-start.3) | collective-permute-done | bytes 524320 | tf_op jit(solution)/shard_map/ppermute | solution.py:21
  136.3 12.9 %collective-permute-done.2 = f32[2,256,256]{1,2,0:T(8,128)} collective-permute-done((f32[2,256,256]{1,2,0:T(8,128)S(1)}, f32[2,256,256]{1,2,0:T(8,128)}, u32[]{:S(2)}, u32[]{:S(2)}) %collective-permute-start.2) | collective-permute-done | bytes 524320 | tf_op jit(solution)/shard_map/ppermute | solution.py:21
  149.2 1.3 fusion.32
  150.6 0.8 copy.23
  151.4 0.8 copy.24
  (9 shorter events, 0.1 us)
Async XLA Ops:
  0.6 76.5 %copy-start = (bf16[256,4096]{1,0:T(8,128)(2,1)S(1)}, bf16[256,4096]{1,0:T(8,128)(2,1)}, u32[]{:S(2)}) copy-start(bf16[256,4096]{1,0:T(8,128)(2,1)} %param.11) | copy-start | bytes 6291460
  3.3 5.0 %copy-start.6 = (bf16[256,256]{1,0:T(8,128)(2,1)S(1)}, bf16[256,256]{1,0:T(8,128)(2,1)}, u32[]{:S(2)}) copy-start(bf16[256,256]{1,0:T(8,128)(2,1)} %param.9) | copy-start | bytes 393220
  3.3 5.0 %copy-start.7 = (bf16[256,256]{1,0:T(8,128)(2,1)S(1)}, bf16[256,256]{1,0:T(8,128)(2,1)}, u32[]{:S(2)}) copy-start(bf16[256,256]{1,0:T(8,128)(2,1)} %param.8) | copy-start | bytes 393220
  3.3 15.5 %copy-start.10 = (s32[128,128]{1,0:T(8,128)S(1)}, s32[128,128]{1,0:T(8,128)}, u32[]{:S(2)}) copy-start(s32[128,128]{1,0:T(8,128)} %param.12) | copy-start | bytes 196612
  3.3 73.8 %all-to-all-start = ((bf16[8,256,512]{1,2,0:T(8,128)(2,1)}), bf16[8,256,512]{1,2,0:T(8,128)(2,1)}, u32[]{:S(2)}, u32[]{:S(2)}) async-start(bf16[8,256,512]{1,2,0:T(8,128)(2,1)} %stack.32), calls=%async_computation | async-start | bytes 4194304 | tf_op jit(solution)/shard_map/all_to_all | solution.py:76
  8.4 66.5 %collective-permute-start.1 = (bf16[2,256,256]{2,1,0:T(8,128)(2,1)S(1)}, bf16[2,256,256]{2,1,0:T(8,128)(2,1)S(1)}, u32[]{:S(2)}, u32[]{:S(2)}) collective-permute-start(bf16[2,256,256]{2,1,0:T(8,128)(2,1)S(1)} %pad_maximum_fusion.1), channel_id=1, source_target_pairs={{0,8},{8,16},{16,24},{24,32},{32,40},{40,48},{48,56},{56,64},{64,7... | collective-permute-start | bytes 786440 | tf_op jit(solution)/shard_map/ppermute | solution.py:21
  12.7 62.2 %collective-permute-start = (bf16[2,256,256]{2,1,0:T(8,128)(2,1)S(1)}, bf16[2,256,256]{2,1,0:T(8,128)(2,1)S(1)}, u32[]{:S(2)}, u32[]{:S(2)}) collective-permute-start(bf16[2,256,256]{2,1,0:T(8,128)(2,1)S(1)} %pad_maximum_fusion.1), channel_id=1, source_target_pairs={{0,16},{8,24},{16,32},{24,40},{32,48},{40,56},{48,64},{56,72},{64,... | collective-permute-start | bytes 786440 | tf_op jit(solution)/shard_map/ppermute | solution.py:21
  19.2 55.8 %copy-start.8 = (bf16[256,256]{1,0:T(8,128)(2,1)S(1)}, bf16[256,256]{1,0:T(8,128)(2,1)}, u32[]{:S(2)}) copy-start(bf16[256,256]{1,0:T(8,128)(2,1)} %param.7) | copy-start | bytes 393220
  21.3 53.9 %copy-start.9 = (pred[256,768]{0,1:T(32,128)(4,1)S(1)}, pred[256,768]{0,1:T(32,128)(4,1)}, u32[]{:S(2)}) copy-start(pred[256,768]{0,1:T(32,128)(4,1)} %copy.17) | copy-start | bytes 589828
  74.9 0.9 copy-start.2
  75.8 0.9 copy-start.4
  77.1 2.4 %copy-start.3 = (bf16[2,768,256]{2,1,0:T(8,128)(2,1)S(1)}, bf16[2,768,256]{2,1,0:T(8,128)(2,1)}, u32[]{:S(2)}) copy-start(bf16[2,768,256]{2,1,0:T(8,128)(2,1)} %copy-done.2) | copy-start | bytes 2359300
  80.3 1.1 copy-start.5
  84.9 21.7 %copy-start.1 = (f32[1,768,256]{1,2,0:T(8,128)}, f32[1,768,256]{1,2,0:T(8,128)S(1)}, u32[]{:S(2)}) copy-start(f32[1,768,256]{1,2,0:T(8,128)S(1)} %maximum_bitcast_fusion.1) | copy-start | bytes 2359300
  86.0 50.3 %collective-permute-start.3 = (f32[2,256,256]{1,2,0:T(8,128)}, f32[2,256,256]{1,2,0:T(8,128)}, u32[]{:S(2)}, u32[]{:S(2)}) collective-permute-start(f32[2,256,256]{1,2,0:T(8,128)} %get-tuple-element.17), channel_id=1, source_target_pairs={{16,0},{24,8},{32,16},{40,24},{48,32},{56,40},{64,48},{72,56},{80,... | collective-permute-start | bytes 1572872 | tf_op jit(solution)/shard_map/ppermute | solution.py:21
  93.2 56.1 %collective-permute-start.2 = (f32[2,256,256]{1,2,0:T(8,128)S(1)}, f32[2,256,256]{1,2,0:T(8,128)}, u32[]{:S(2)}, u32[]{:S(2)}) collective-permute-start(f32[2,256,256]{1,2,0:T(8,128)S(1)} %get-tuple-element.16), channel_id=1, source_target_pairs={{8,0},{16,8},{24,16},{32,24},{40,32},{48,40},{56,48},{64,56},{72,6... | collective-permute-start | bytes 1572872 | tf_op jit(solution)/shard_map/ppermute | solution.py:21
